TPU v7x, 32 devices: a whole 2x2x4 slice. The times are simulated.
32 devices in a mesh: sec: 4 (over y, core), ctx: 2 (over x), tp: 4 (over z).
Axes of the slice: x: 2, y: 2, z: 4, core: 2. Of those that a mesh axis runs over, the one named last changes fastest.
Arguments:
- self_query: bfloat16 [1024, 2048], P('ctx', ('sec', 'tp')), may hold values from -6 to 6
- self_key: bfloat16 [1024, 2048], P('ctx', ('sec', 'tp')), may hold values from -6 to 6
- self_value: bfloat16 [1024, 2048], P('ctx', ('sec', 'tp')), may hold values from -6 to 6
- self_gain: float32 [2048], P(('sec', 'tp')), may hold values from 0.5 to 1.5
- self_grad: bfloat16 [1024, 2048], P('ctx', ('sec', 'tp')), may hold values from -6 to 6
- cross_query: bfloat16 [1024, 2048], P('ctx', ('sec', 'tp')), may hold values from -6 to 6
- memory_key: bfloat16 [256, 2048], P(('sec', 'ctx')), may hold values from -6 to 6
- memory_value: bfloat16 [256, 2048], P(('sec', 'ctx')), may hold values from -6 to 6
- cross_gain: float32 [2048], P(('sec', 'tp')), may hold values from 0.5 to 1.5
- cross_grad: bfloat16 [1024, 2048], P('ctx', ('sec', 'tp')), may hold values from -6 to 6
- block_start: int32 [8], replicated, may hold values from 0 to 7, each once
Outputs:
- self_out: bfloat16 [1024, 2048], P('ctx', ('sec', 'tp'))
- cross_out: bfloat16 [1024, 2048], P('ctx', ('sec', 'tp'))
- query_grad: bfloat16 [1024, 2048], P('ctx', ('sec', 'tp'))
- key_grad: bfloat16 [1024, 2048], P('ctx', ('sec', 'tp'))
- value_grad: bfloat16 [1024, 2048], P('ctx', ('sec', 'tp'))
- cross_query_grad: bfloat16 [1024, 2048], P('ctx', ('sec', 'tp'))
- memory_key_grad: bfloat16 [256, 2048], P(('sec', 'ctx'))
- memory_value_grad: bfloat16 [256, 2048], P(('sec', 'ctx'))
Inputs may be any that keep to these rules, and one draw needn't show every extreme that they name: `block_start`: every number appears once.
All inputs are finite; a program needn't handle non-finite values.
Results may differ from a plain program's by a relative error of at most 0.015.
Values may be sent and summed in bfloat16 or wider, within the bound.
No kernel may reach another device: no remote copies, remote signals or barrier semaphores. Data moves between devices by JAX's collectives and lax.ppermute only.
A program may use at most 64 MiB of HBM per device.

v0:
```python
import math
import jax
import jax.numpy as jnp
from jax import lax
from jax.sharding import PartitionSpec as P

HEADS = 16
HEAD_DIM = 128
EPS = 1e-06
NEG_FILL = -1e30


def split_heads(matrix):
    return matrix.reshape(matrix.shape[0], matrix.shape[1] // HEAD_DIM, HEAD_DIM)


def frame_positions(block_start, first_row, row_count, block_rows):
    row_ids = first_row + jnp.arange(row_count, dtype=jnp.int32)
    owners = row_ids // block_rows
    lookup = owners[:, None] == jnp.arange(block_start.shape[0], dtype=jnp.int32)[None, :]
    starts = jnp.sum(jnp.where(lookup, block_start[None, :], 0), axis=1)
    return starts * block_rows + row_ids % block_rows


def skipped(key_positions, query_positions):
    return jnp.min(key_positions) > jnp.max(query_positions)


def masked_scores(queries, key_block, key_positions, query_positions, filler):
    scores = jnp.einsum("qhd,khd->hqk", queries, key_block, preferred_element_type=jnp.float32) * (
        1.0 / math.sqrt(HEAD_DIM)
    )
    if key_positions is None:
        return scores
    return jnp.where(key_positions[None, None, :] > query_positions[None, :, None], filler, scores)


def fold_softmax(carried, pieces, queries, query_positions, position_of):
    row_top, row_total, key_store, value_store = carried
    key_piece, value_piece = pieces
    row_count = key_piece.shape[0]
    key_store = key_piece
    value_store = value_piece
    block_length = math.gcd(row_count, 1024)

    def fold_visit(turn_index, running):
        offset = turn_index * block_length
        key_block = split_heads(lax.dynamic_slice_in_dim(key_piece, offset, block_length, 0))
        key_positions = None if position_of is None else position_of(offset, block_length)

        def update(current):
            old_top, old_total = current
            scores = masked_scores(queries, key_block, key_positions, query_positions, NEG_FILL)
            new_top = jnp.maximum(old_top, jnp.max(scores, axis=2))
            new_total = old_total * jnp.exp(old_top - new_top) + jnp.sum(
                jnp.exp(scores - new_top[:, :, None]), axis=2
            )
            return (new_top, new_total)

        if key_positions is None:
            return update(running)
        return lax.cond(
            skipped(key_positions, query_positions), lambda unused: unused, update, running
        )

    row_top, row_total = lax.fori_loop(
        0, row_count // block_length, fold_visit, (row_top, row_total)
    )
    return (row_top, row_total, key_store, value_store)


def attend(queries, log_total, key_store, value_store, query_positions, position_of):
    key_count = key_store.shape[0]
    block_length = math.gcd(key_count, 512)

    def attend_visit(turn_index, running):
        offset = turn_index * block_length
        key_block = split_heads(lax.dynamic_slice_in_dim(key_store, offset, block_length, 0))
        value_block = split_heads(lax.dynamic_slice_in_dim(value_store, offset, block_length, 0))
        key_positions = None if position_of is None else position_of(offset, block_length)

        def update(current):
            scores = masked_scores(queries, key_block, key_positions, query_positions, -jnp.inf)
            weights = jnp.exp(scores - log_total[:, :, None]).astype(jnp.bfloat16)
            return current + jnp.einsum(
                "hqk,khd->qhd", weights, value_block, preferred_element_type=jnp.float32
            )

        if key_positions is None:
            return update(running)
        return lax.cond(
            skipped(key_positions, query_positions), lambda unused: unused, update, running
        )

    result = lax.fori_loop(
        0, key_count // block_length, attend_visit, jnp.zeros(queries.shape, jnp.float32)
    )
    return result.reshape(queries.shape[0], queries.shape[1] * HEAD_DIM)


def score_parts(
    queries, cotangent, log_total, row_delta, key_block, value_block, key_positions, query_positions
):
    scores = masked_scores(queries, key_block, key_positions, query_positions, -jnp.inf)
    weights = jnp.exp(scores - log_total[:, :, None])
    products = jnp.einsum(
        "qhd,khd->hqk", cotangent, value_block, preferred_element_type=jnp.float32
    )
    score_grad = (weights * (products - row_delta[:, :, None])).astype(jnp.bfloat16)
    return (weights, score_grad)


def key_side_terms(queries, cotangent, weights, score_grad):
    key_part = jnp.einsum(
        "hqk,qhd->khd", score_grad, queries, preferred_element_type=jnp.float32
    ) * (1.0 / math.sqrt(HEAD_DIM))
    value_part = jnp.einsum(
        "hqk,qhd->khd", weights.astype(jnp.bfloat16), cotangent, preferred_element_type=jnp.float32
    )
    rows_here = key_part.shape[0]
    return jnp.concatenate(
        [key_part.reshape(rows_here, -1), value_part.reshape(rows_here, -1)], axis=1
    )


def joint_backward(
    queries, cotangent, log_total, row_delta, key_store, value_store, query_positions, position_of
):
    key_count = key_store.shape[0]
    block_length = math.gcd(key_count, 512)
    columns = queries.shape[1] * HEAD_DIM

    def joint_visit(turn_index, running):
        offset = turn_index * block_length
        key_block = split_heads(lax.dynamic_slice_in_dim(key_store, offset, block_length, 0))
        value_block = split_heads(lax.dynamic_slice_in_dim(value_store, offset, block_length, 0))
        key_positions = None if position_of is None else position_of(offset, block_length)

        def update(current):
            query_sum, key_terms = current
            weights, score_grad = score_parts(
                queries,
                cotangent,
                log_total,
                row_delta,
                key_block,
                value_block,
                key_positions,
                query_positions,
            )
            query_sum = query_sum + jnp.einsum(
                "hqk,khd->qhd", score_grad, key_block, preferred_element_type=jnp.float32
            ) * (1.0 / math.sqrt(HEAD_DIM))
            key_terms = lax.dynamic_update_slice_in_dim(
                key_terms, key_side_terms(queries, cotangent, weights, score_grad), offset, 0
            )
            return (query_sum, key_terms)

        if key_positions is None:
            return update(running)
        return lax.cond(
            skipped(key_positions, query_positions), lambda unused: unused, update, running
        )

    start_value = (
        jnp.zeros(queries.shape, jnp.float32),
        jnp.zeros((key_count, 2 * columns), jnp.float32),
    )
    query_sum, key_terms = lax.fori_loop(0, key_count // block_length, joint_visit, start_value)
    return (query_sum.reshape(queries.shape[0], columns), key_terms)


def backprop_norm(attended, lifted, row_scale, row_slope):
    return (
        row_scale[:, None] * (lifted - attended * (row_scale * row_scale * row_slope)[:, None])
    ).astype(jnp.bfloat16)


def head_delta(attended_grad, attended):
    return jnp.sum(
        (attended_grad.astype(jnp.float32) * attended).reshape(attended.shape[0], -1, HEAD_DIM),
        axis=2,
    ).T


def per_device(
    self_query,
    self_key,
    self_value,
    self_gain,
    self_grad,
    cross_query,
    memory_key,
    memory_value,
    cross_gain,
    cross_grad,
    block_start,
):
    frames_dev, columns = self_query.shape
    quarter_rows = frames_dev // 4
    full_width = HEADS * HEAD_DIM
    context_count = lax.axis_size("ctx")
    section_count = lax.axis_size("sec")
    tensor_count = lax.axis_size("tp")
    memory_rows = memory_key.shape[0]
    head_count = columns // HEAD_DIM
    own_positions = frame_positions(
        block_start, lax.axis_index("ctx") * frames_dev, frames_dev, quarter_rows
    )

    def position_of(first_row, row_count):
        return frame_positions(block_start, first_row, row_count, quarter_rows)

    own_queries = split_heads(self_query)
    empty_top = jnp.full((head_count, frames_dev), NEG_FILL, jnp.float32)
    empty_total = jnp.zeros((head_count, frames_dev), jnp.float32)
    frame_store = jnp.zeros((frames_dev * context_count, columns), jnp.bfloat16)
    self_top, self_sum, key_store, value_store = fold_softmax(
        (empty_top, empty_total, frame_store, frame_store),
        (
            lax.all_gather(self_key, "ctx", axis=0, tiled=True),
            lax.all_gather(self_value, "ctx", axis=0, tiled=True),
        ),
        own_queries,
        own_positions,
        position_of,
    )
    self_log_total = self_top + jnp.log(self_sum)
    self_attended = attend(
        own_queries, self_log_total, key_store, value_store, own_positions, position_of
    )

    def own_heads(memory):
        grouped = memory.reshape(memory_rows, section_count, tensor_count, columns)
        picked = lax.dynamic_slice_in_dim(grouped, lax.axis_index("tp"), 1, 2)
        return picked.reshape(memory_rows, section_count, columns)

    memory_keys, memory_values = (
        lax.all_to_all(own_heads(memory_key), "sec", split_axis=1, concat_axis=0, tiled=True),
        lax.all_to_all(own_heads(memory_value), "sec", split_axis=1, concat_axis=0, tiled=True),
    )
    section_rows = section_count * memory_rows
    memory_keys = memory_keys.reshape(section_rows, columns)
    memory_values = memory_values.reshape(section_rows, columns)
    cross_queries = split_heads(cross_query)
    memory_store = jnp.zeros((section_rows * context_count, columns), jnp.bfloat16)
    cross_top, cross_sum, memory_key_store, memory_value_store = fold_softmax(
        (empty_top, empty_total, memory_store, memory_store),
        (
            lax.all_gather(memory_keys, "ctx", axis=0, tiled=True),
            lax.all_gather(memory_values, "ctx", axis=0, tiled=True),
        ),
        cross_queries,
        own_positions,
        None,
    )
    cross_log_total = cross_top + jnp.log(cross_sum)
    cross_attended = attend(
        cross_queries, cross_log_total, memory_key_store, memory_value_store, own_positions, None
    )
    self_lifted = self_gain[None, :] * self_grad.astype(jnp.float32)
    cross_lifted = cross_gain[None, :] * cross_grad.astype(jnp.float32)
    self_squares = jnp.sum(self_attended * self_attended, axis=1)
    cross_squares = jnp.sum(cross_attended * cross_attended, axis=1)
    self_square_sum, cross_square_sum = lax.psum((self_squares, cross_squares), ("sec", "tp"))
    self_scale = lax.rsqrt(self_square_sum / full_width + EPS)
    cross_scale = lax.rsqrt(cross_square_sum / full_width + EPS)
    self_out = (self_gain[None, :] * self_attended * self_scale[:, None]).astype(jnp.bfloat16)
    cross_out = (cross_gain[None, :] * cross_attended * cross_scale[:, None]).astype(jnp.bfloat16)
    self_slope_sum, cross_slope_sum = lax.psum(
        (
            jnp.sum(self_lifted * self_attended, axis=1),
            jnp.sum(cross_lifted * cross_attended, axis=1),
        ),
        ("sec", "tp"),
    )
    self_attended_grad = backprop_norm(
        self_attended, self_lifted, self_scale, self_slope_sum / full_width
    )
    cross_attended_grad = backprop_norm(
        cross_attended, cross_lifted, cross_scale, cross_slope_sum / full_width
    )
    self_delta = head_delta(self_attended_grad, self_attended)
    self_cotangent = split_heads(self_attended_grad)
    query_sum, all_terms = joint_backward(
        own_queries,
        self_cotangent,
        self_log_total,
        self_delta,
        key_store,
        value_store,
        own_positions,
        position_of,
    )
    query_grad = query_sum.astype(jnp.bfloat16)
    key_terms = lax.psum_scatter(
        all_terms.astype(jnp.bfloat16), "ctx", scatter_dimension=0, tiled=True
    ).astype(jnp.float32)
    key_grad = key_terms[:, :columns].astype(jnp.bfloat16)
    value_grad = key_terms[:, columns:].astype(jnp.bfloat16)
    cross_delta = head_delta(cross_attended_grad, cross_attended)
    cross_query_sum, memory_terms = joint_backward(
        cross_queries,
        split_heads(cross_attended_grad),
        cross_log_total,
        cross_delta,
        memory_key_store,
        memory_value_store,
        None,
        None,
    )
    cross_query_grad = cross_query_sum.astype(jnp.bfloat16)
    memory_sums = lax.psum_scatter(
        memory_terms.astype(jnp.bfloat16), "ctx", scatter_dimension=0, tiled=True
    )
    rounded = memory_sums.reshape(section_rows, 2, 1, 1, columns)
    returned = lax.all_to_all(rounded, "sec", split_axis=0, concat_axis=2, tiled=True)
    complete = lax.all_gather(returned, "tp", axis=3, tiled=True).reshape(
        memory_rows, 2, section_count * tensor_count * columns
    )
    return (
        self_out,
        cross_out,
        query_grad,
        key_grad,
        value_grad,
        cross_query_grad,
        complete[:, 0],
        complete[:, 1],
    )


def solution(mesh):
    return jax.shard_map(
        per_device,
        mesh=mesh,
        in_specs=(
            P("ctx", ("sec", "tp")),
            P("ctx", ("sec", "tp")),
            P("ctx", ("sec", "tp")),
            P(("sec", "tp")),
            P("ctx", ("sec", "tp")),
            P("ctx", ("sec", "tp")),
            P(("sec", "ctx"), None),
            P(("sec", "ctx"), None),
            P(("sec", "tp")),
            P("ctx", ("sec", "tp")),
            P(),
        ),
        out_specs=(
            P("ctx", ("sec", "tp")),
            P("ctx", ("sec", "tp")),
            P("ctx", ("sec", "tp")),
            P("ctx", ("sec", "tp")),
            P("ctx", ("sec", "tp")),
            P("ctx", ("sec", "tp")),
            P(("sec", "ctx"), None),
            P(("sec", "ctx"), None),
        ),
        check_vma=False,
    )
```

profile of v0, /device:TPU:0, one launch (start us, length us, event | category | flops | bytes accessed | tf_op | source)
XLA Modules:
  0.0 131.9 jit_solution(3163522244689246081)
XLA Ops:
  7.2 1.0 reshape.417
  8.9 4.3 %all-to-all-start.1 = ((bf16[32,4,128]{2,0,1:T(8,128)(2,1)}), bf16[32,4,128]{2,0,1:T(8,128)(2,1)S(1)}, u32[]{:S(2)}, u32[]{:S(2)}) async-start(bf16[32,4,128]{2,0,1:T(8,128)(2,1)} %bitcast.165), calls=%async_computation.1 | async-start | bytes 65536 | tf_op jit(solution)/shard_map/all_to_all | solution.py:239
  13.2 1.0 reshape.414
  14.2 0.7 select_reduce_fusion.3
  15.6 7.0 %all_gather.16 = bf16[1024,128]{1,0:T(8,128)(2,1)S(1)} all-gather(bf16[512,128]{1,0:T(8,128)(2,1)} %param.22), channel_id=1, replica_groups=mesh['sec'=4,'ctx'=2,'tp'=4] {'ctx'}, dimensions={0}, use_global_device_ids=true | all-gather | bytes 393216 | tf_op jit(solution)/shard_map/all_gather | solution.py:221
  25.3 6.2 %all_gather.15 = bf16[1024,128]{1,0:T(8,128)(2,1)S(1)} all-gather(bf16[512,128]{1,0:T(8,128)(2,1)} %param.23), channel_id=1, replica_groups=mesh['sec'=4,'ctx'=2,'tp'=4] {'ctx'}, dimensions={0}, use_global_device_ids=true | all-gather | bytes 393216 | tf_op jit(solution)/shard_map/all_gather | solution.py:222
  31.4 2.2 %conditional.3 = (f32[1,512]{1,0:T(1,128)S(1)}, f32[1,512]{1,0:T(1,128)S(1)}) conditional(s32[]{:T(128)} %convert_element_type.106, (s32[1024]{0:T(1024)S(1)}, s32[512]{0:T(512)S(1)}, bf16[512,1,128]{2,0,1:T(8,128)(2,1)}, bf16[1024,128]{1,0:T(8,128)(2,1)S(1)}, f32[1,512]{1,0:T(1,128)S(1)}, /*index=5*/f32[1,512]{1,0:T(1,128)S(1)}) %tuple.182, ...), branch_computations={%region_4.7_spmd, %region_7.8_spmd} | conditional | flops 138937344 | bytes 4622352 | solution.py:62
  31.4 1.5 %fusion = (f32[512]{0:T(512)S(1)}, f32[512,1024]{1,0:T(8,128)S(1)}) fusion(s32[1024]{0:T(1024)S(1)} %get-tuple-element.800, s32[512]{0:T(512)S(1)} %get-tuple-element.801, bf16[1024,128]{1,0:T(8,128)(2,1)S(1)} %get-tuple-element.803, bf16[512,1,128]{2,0,1:T(8,128)(2,1)} %get-tuple-element.802), kind=kOutput, calls=%fused_computation.2 | convolution fusion | flops 136314368 | bytes 2498560 | tf_op jit(solution)/shard_map/while/body/eval_jaxpr/cond/branch_0_fun/qhd,khd->hqk/dot_general | solution.py:30
  33.7 7.2 %while.24 = (s32[]{:T(128)}, f32[512,1,128]{0,2,1:T(8,128)S(1)}, s32[8]{0:T(128)S(1)}, s32[]{:T(128)}, bf16[1024,128]{1,0:T(8,128)(2,1)S(1)}, /*index=5*/s32[512...) while((s32[]{:T(128)}, f32[512,1,128]{0,2,1:T(8,128)S(1)}, ...), condition=%wide.region_13.14_spmd, body=%wide.region_8.13_spmd.sunk | while | flops 135621632 | bytes 935197 | solution.py:95
  35.7 1.5 %conditional.6 = (f32[512,1,128]{0,2,1:T(8,128)S(1)}) conditional(s32[]{:T(128)} %convert_element_type.172, (s32[]{:T(128)}, bf16[1024,128]{1,0:T(8,128)(2,1)S(1)}, s32[512]{0:T(512)S(1)}, s32[512]{0:T(512)S(1)}, bf16[1024,128]{1,0:T(8,128)(2,1)S(1)}, /*index=5*/bf16[512,1,128]{2,0,1:T(8,128)(2,1)}, f32[1,512]{1,0:T(1,128)S(1)}, ...), branch_computations={%region_11.11_spmd, %region_12.12_spmd} | conditional | flops 135593984 | bytes 924714 | solution.py:91
  35.8 1.5 %fusion.10 = f32[512,1,128]{0,2,1:T(8,128)S(1)} fusion(f32[512,1,128]{0,2,1:T(8,128)S(1)} %get-tuple-element.807, f32[512]{0:T(512)S(1)} %bitcast.178, s32[512]{0:T(512)S(1)} %get-tuple-element.811, s32[512]{0:T(512)S(1)} %get-tuple-element.810, bf16[512,1,128]{2,0,1:T(8,128)(2,1)} %get-tuple-element.813, bf16[1024,128]{1,0:T(8,128)(2,1)S(1)} %get-tuple-element.812, ...), kind=kOutput, calls=%fused_computation.14 | convolution fusion | flops 135593984 | bytes 924672 | tf_op jit(solution)/shard_map/while/body/eval_jaxpr/cond/branch_0_fun/hqk,khd->qhd/dot_general | solution.py:85
  39.3 1.5 %conditional.6 = (f32[512,1,128]{0,2,1:T(8,128)S(1)}) conditional(s32[]{:T(128)} %convert_element_type.172, (s32[]{:T(128)}, bf16[1024,128]{1,0:T(8,128)(2,1)S(1)}, s32[512]{0:T(512)S(1)}, s32[512]{0:T(512)S(1)}, bf16[1024,128]{1,0:T(8,128)(2,1)S(1)}, /*index=5*/bf16[512,1,128]{2,0,1:T(8,128)(2,1)}, f32[1,512]{1,0:T(1,128)S(1)}, ...), branch_computations={%region_11.11_spmd, %region_12.12_spmd} | conditional | flops 135593984 | bytes 924714 | solution.py:91
  39.3 1.5 %fusion.10 = f32[512,1,128]{0,2,1:T(8,128)S(1)} fusion(f32[512,1,128]{0,2,1:T(8,128)S(1)} %get-tuple-element.807, f32[512]{0:T(512)S(1)} %bitcast.178, s32[512]{0:T(512)S(1)} %get-tuple-element.811, s32[512]{0:T(512)S(1)} %get-tuple-element.810, bf16[512,1,128]{2,0,1:T(8,128)(2,1)} %get-tuple-element.813, bf16[1024,128]{1,0:T(8,128)(2,1)S(1)} %get-tuple-element.812, ...), kind=kOutput, calls=%fused_computation.14 | convolution fusion | flops 135593984 | bytes 924672 | tf_op jit(solution)/shard_map/while/body/eval_jaxpr/cond/branch_0_fun/hqk,khd->qhd/dot_general | solution.py:85
  42.1 3.3 %all-to-all-start = ((bf16[32,4,128]{2,0,1:T(8,128)(2,1)}), bf16[32,4,128]{2,0,1:T(8,128)(2,1)S(1)}, u32[]{:S(2)}, u32[]{:S(2)}) async-start(bf16[32,4,128]{2,0,1:T(8,128)(2,1)} %bitcast.166), calls=%async_computation | async-start | bytes 65536 | tf_op jit(solution)/shard_map/all_to_all | solution.py:240
  45.4 4.6 %all_gather.18 = bf16[256,128]{1,0:T(8,128)(2,1)S(1)} all-gather(bf16[128,128]{1,0:T(8,128)(2,1)S(1)} %bitcast.172), channel_id=1, replica_groups=mesh['sec'=4,'ctx'=2,'tp'=4] {'ctx'}, dimensions={0}, use_global_device_ids=true | all-gather | bytes 98304 | tf_op jit(solution)/shard_map/all_gather | solution.py:250
  50.4 4.6 %all_gather.17 = bf16[256,128]{1,0:T(8,128)(2,1)S(1)} all-gather(bf16[128,128]{1,0:T(8,128)(2,1)S(1)} %bitcast.173), channel_id=1, replica_groups=mesh['sec'=4,'ctx'=2,'tp'=4] {'ctx'}, dimensions={0}, use_global_device_ids=true | all-gather | bytes 98304 | tf_op jit(solution)/shard_map/all_gather | solution.py:251
  55.2 32.7 %all-reduce = (f32[512]{0:T(512)S(1)}, f32[512]{0:T(512)S(1)}, f32[512]{0:T(512)S(1)}, f32[512]{0:T(512)S(1)}) all-reduce(f32[512]{0:T(512)S(1)} %get-tuple-element.924, f32[512]{0:T(512)S(1)} %get-tuple-element.922, f32[512]{0:T(512)S(1)} %get-tuple-element.923, ...), channel_id=1, replica_groups=mesh['sec'=4,'ctx'=2,'tp'=4] {'sec','tp'}, use_global_device_ids=true, to_apply=%region_15.16 | all-reduce | flops 2048 | bytes 16384 | tf_op jit(solution)/shard_map/psum | solution.py:265
  88.9 0.8 copy.74
  89.7 0.9 fusion.68
  90.7 7.5 %while.25 = (s32[]{:T(128)}, f32[512,1,128]{0,2,1:T(8,128)S(1)}, bf16[1024,256]{0,1:T(8,128)(2,1)S(1)}, s32[8]{0:T(128)S(1)}, s32[]{:T(128)}, /*index=5*/bf16[10...) while((s32[]{:T(128)}, f32[512,1,128]{0,2,1:T(8,128)S(1)}, ...), condition=%wide.region_28.29_spmd, body=%wide.region_23.28_spmd.sunk | while | flops 338455552 | bytes 6965629 | solution.py:169
  92.7 1.7 %conditional.7 = ((f32[512,1,128]{0,2,1:T(8,128)S(1)}, bf16[1024,256]{0,1:T(8,128)(2,1)S(1)})) conditional(s32[]{:T(128)} %convert_element_type.173, (s32[]{:T(128)}, bf16[1024,128]{1,0:T(8,128)(2,1)S(1)}, s32[512]{0:T(512)S(1)}, s32[512]{0:T(512)S(1)}, bf16[512,1,128]{2,0,1:T(8,128)(2,1)S(1)}, /*index=5*/f32[1,512]{1,0:T(1,128)S(1)}, ...), branch_computations={%region_26.26_spmd, %region_27.27_spmd} | conditional | flops 338427904 | bytes 6955082 | solution.py:161
  96.5 1.7 %conditional.7 = ((f32[512,1,128]{0,2,1:T(8,128)S(1)}, bf16[1024,256]{0,1:T(8,128)(2,1)S(1)})) conditional(s32[]{:T(128)} %convert_element_type.173, (s32[]{:T(128)}, bf16[1024,128]{1,0:T(8,128)(2,1)S(1)}, s32[512]{0:T(512)S(1)}, s32[512]{0:T(512)S(1)}, bf16[512,1,128]{2,0,1:T(8,128)(2,1)S(1)}, /*index=5*/f32[1,512]{1,0:T(1,128)S(1)}, ...), branch_computations={%region_26.26_spmd, %region_27.27_spmd} | conditional | flops 338427904 | bytes 6955082 | solution.py:161
  98.2 1.0 copy.64
  99.2 0.9 copy.75
  100.2 0.8 copy.67
  101.0 3.3 %all-to-all-start.2 = ((bf16[128,2,1,1,128]{4,1,3,2,0:T(2,128)(2,1)}), bf16[128,2,1,1,128]{4,1,3,2,0:T(2,128)(2,1)S(1)}, u32[]{:S(2)}, u32[]{:S(2)}) async-start(bf16[128,2,1,1,128]{4,1,3,2,0:T(2,128)(2,1)} %copy.67), calls=%async_computation.3 | async-start | bytes 131072 | tf_op jit(solution)/shard_map/all_to_all | solution.py:317
  104.5 0.8 copy.72
  105.2 0.8 copy.63
  106.0 0.8 copy.71
  106.8 1.6 %all-to-all-done.2 = bf16[128,2,1,1,128]{4,1,3,2,0:T(2,128)(2,1)S(1)} async-done(((bf16[128,2,1,1,128]{4,1,3,2,0:T(2,128)(2,1)}), bf16[128,2,1,1,128]{4,1,3,2,0:T(2,128)(2,1)S(1)}, u32[]{:S(2)}, u32[]{:S(2)}) %all-to-all-start.2) | async-done | bytes 65568 | tf_op jit(solution)/shard_map/all_to_all | solution.py:317
  108.4 13.9 %all-gather = bf16[32,2,4,4,1,128]{5,0,4,2,1,3:T(8,128)(2,1)S(1)} all-gather(bf16[32,2,4,1,1,128]{5,0,4,2,1,3:T(8,128)(2,1)S(1)} %bitcast.169), channel_id=2, replica_groups=mesh['sec'=4,'ctx'=2,'tp'=4] {'tp'}, dimensions={3}, use_global_device_ids=true | all-gather | bytes 327680 | tf_op jit(solution)/shard_map/all_gather | solution.py:318
  123.3 1.7 %fusion.90 = (bf16[512,128]{1,0:T(8,128)(2,1)}, bf16[512,128]{1,0:T(8,128)(2,1)}) fusion(bf16[512,256]{1,0:T(8,128)(2,1)} %reduce-scatter.5.cloned.1.call-done), kind=kLoop, calls=%fused_computation.160 | loop fusion | bytes 524288 | tf_op jit(solution)/shard_map/slice | solution.py:300
  (83 shorter events, 13.9 us)
Async XLA Ops:
  7.2 42.8 %copy-start = (bf16[512,128]{1,0:T(8,128)(2,1)S(1)}, bf16[512,128]{1,0:T(8,128)(2,1)}, u32[]{:S(2)}) copy-start(bf16[512,128]{1,0:T(8,128)(2,1)} %param.26) | copy-start | bytes 393220
  8.9 33.2 %all-to-all-start.1 = ((bf16[32,4,128]{2,0,1:T(8,128)(2,1)}), bf16[32,4,128]{2,0,1:T(8,128)(2,1)S(1)}, u32[]{:S(2)}, u32[]{:S(2)}) async-start(bf16[32,4,128]{2,0,1:T(8,128)(2,1)} %bitcast.165), calls=%async_computation.1 | async-start | bytes 65536 | tf_op jit(solution)/shard_map/all_to_all | solution.py:239
  31.4 2.2 %copy-start.4 = (s32[8]{0:T(128)S(1)}, s32[8]{0:T(128)}, u32[]{:S(2)}) copy-start(s32[8]{0:T(128)} %param.31) | copy-start | bytes 100
  33.6 7.4 %copy-start.2 = (bf16[512,128]{1,0:T(8,128)(2,1)S(1)}, bf16[512,128]{1,0:T(8,128)(2,1)}, u32[]{:S(2)}) copy-start(bf16[512,128]{1,0:T(8,128)(2,1)} %param.25) | copy-start | bytes 393220
  33.6 7.4 %copy-start.6 = (f32[128]{0:T(128)S(1)}, f32[128]{0:T(128)}, u32[]{:S(2)}) copy-start(f32[128]{0:T(128)} %param.24) | copy-start | bytes 1540
  33.7 8.3 %copy-start.3 = (bf16[512,128]{1,0:T(8,128)(2,1)S(1)}, bf16[512,128]{1,0:T(8,128)(2,1)}, u32[]{:S(2)}) copy-start(bf16[512,128]{1,0:T(8,128)(2,1)} %param.30) | copy-start | bytes 393220
  40.9 14.1 %copy-start.5 = (f32[128]{0:T(128)S(1)}, f32[128]{0:T(128)}, u32[]{:S(2)}) copy-start(f32[128]{0:T(128)} %param.29) | copy-start | bytes 1540
  42.1 8.3 %all-to-all-start = ((bf16[32,4,128]{2,0,1:T(8,128)(2,1)}), bf16[32,4,128]{2,0,1:T(8,128)(2,1)S(1)}, u32[]{:S(2)}, u32[]{:S(2)}) async-start(bf16[32,4,128]{2,0,1:T(8,128)(2,1)} %bitcast.166), calls=%async_computation | async-start | bytes 65536 | tf_op jit(solution)/shard_map/all_to_all | solution.py:240
  45.4 53.9 %reduce-scatter.7.cloned.1.call-start = ((), (), s32[]{:S(2)}) async-start(), calls=%async_computation.6 | async-start | bytes 196608
  88.1 2.5 %copy-start.1 = (bf16[512,1,128]{2,0,1:T(8,128)(2,1)S(1)}, bf16[512,1,128]{2,0,1:T(8,128)(2,1)}, u32[]{:S(2)}) copy-start(bf16[512,1,128]{2,0,1:T(8,128)(2,1)} %get-tuple-element.1228) | copy-start | bytes 393220
  89.7 33.7 %reduce-scatter.5.cloned.1.call-start = ((), (), s32[]{:S(2)}) async-start(), calls=%async_computation.5 | async-start | bytes 786432 | tf_op jit(solution)/shard_map/reduce_scatter | solution.py:296
  101.0 7.4 %all-to-all-start.2 = ((bf16[128,2,1,1,128]{4,1,3,2,0:T(2,128)(2,1)}), bf16[128,2,1,1,128]{4,1,3,2,0:T(2,128)(2,1)S(1)}, u32[]{:S(2)}, u32[]{:S(2)}) async-start(bf16[128,2,1,1,128]{4,1,3,2,0:T(2,128)(2,1)} %copy.67), calls=%async_computation.3 | async-start | bytes 131072 | tf_op jit(solution)/shard_map/all_to_all | solution.py:317
Sparse Core Ops, SparseCore 0:
  89.8 8.1 reduce-scatter.6
  100.3 14.6 reduce-scatter.4
where the time goes:
time: 133 us; the launch traced here: 132 us
  blocking collectives  68.9 us (52%)
  between operations  15.7 us (12%)
  local copies, waits for them, and re-layouts  12.3 us (9%)
  starting transfers between devices  10.9 us (8%)
  matrix products  9.01 us (7%)
  other arithmetic  7.87 us (6%)
  loops' own time  5.55 us (4%)
  waiting for transfers between devices  1.65 us (1%)
    psum x1, blocking collectives, per_device(): lax.psum((self_squares, cross_squares), ('sec', 'tp'))  32.7 us
    all_gather x1, blocking collectives, per_device(): lax.all_gather(returned, 'tp', axis=3, tiled=True)  13.9 us
    all_gather x1, blocking collectives, per_device(): lax.all_gather(self_key, 'ctx', axis=0, tiled=True)  7.02 us
    all_gather x1, blocking collectives, per_device(): lax.all_gather(self_value, 'ctx', axis=0, tiled=True)  6.16 us
    all_gather x1, blocking collectives, per_device(): lax.all_gather(memory_keys, 'ctx', axis=0, tiled=True)  4.58 us
    all_gather x1, blocking collectives, per_device(): lax.all_gather(memory_values, 'ctx', axis=0, tiled=True)  4.58 us
    all_to_all x1, starting transfers between devices, per_device(): lax.all_to_all(own_heads(memory_key), 'sec', split_axis=1, concat_axis=0,...  4.26 us
    unnamed x19, local copies, waits for them, and re-layouts  3.39 us
  transfers between devices with their start and end apart: 5, of which 1 were waited for; matrix products, arithmetic and copies ran while one was open for 18% of the time, Pallas kernels for 0%

commit v1 on v0

--- a/solution.py
+++ b/solution.py
@@ -8,6 +8,22 @@
 HEAD_DIM = 128
 EPS = 1e-06
 NEG_FILL = -1e30
+
+
+def ring_gather(x, axis, dim):
+    ways, here, turn = (lax.axis_size(axis), lax.axis_index(axis), x.shape[dim])
+    dims = [n * ways if d == dim else n for d, n in enumerate(x.shape)]
+    full = lax.dynamic_update_slice_in_dim(jnp.zeros(dims, x.dtype), x, here * turn, axis=dim)
+    going_up = going_down = x
+    for far in range(1, ways // 2 + 1):
+        going_up = lax.ppermute(going_up, axis, [(d, (d + 1) % ways) for d in range(ways)])
+        full = lax.dynamic_update_slice_in_dim(full, going_up, (here - far) % ways * turn, axis=dim)
+        if 2 * far < ways:
+            going_down = lax.ppermute(going_down, axis, [(d, (d - 1) % ways) for d in range(ways)])
+            full = lax.dynamic_update_slice_in_dim(
+                full, going_down, (here + far) % ways * turn, axis=dim
+            )
+    return full
 
 
 def split_heads(matrix):
@@ -315,7 +331,7 @@
     )
     rounded = memory_sums.reshape(section_rows, 2, 1, 1, columns)
     returned = lax.all_to_all(rounded, "sec", split_axis=0, concat_axis=2, tiled=True)
-    complete = lax.all_gather(returned, "tp", axis=3, tiled=True).reshape(
+    complete = ring_gather(returned, "tp", 3).reshape(
         memory_rows, 2, section_count * tensor_count * columns
     )
     return (

time: 133 us -> 137 us (1.030)
  local copies, waits for them, and re-layouts: 12.3 us -> 22.5 us
  blocking collectives: 68.9 us -> 61.6 us
    all_gather x1 -> x0, blocking collectives: 13.9 us -> none  [per_device(): lax.all_gather(returned, 'tp', axis=3, tiled=True)]
    dynamic_update_slice x0 -> x4, local copies, waits for them, and re-layouts: none -> 10.6 us  [the longest x2 5.29 us: ring_gather(): lax.dynamic_update_slice_in_dim(full, going_up, (here - far) % ways * tur...]
    all_to_all x0 -> x1, blocking collectives: none -> 6.49 us  [per_device(): lax.all_to_all(rounded, 'sec', split_axis=0, concat_axis=2, tiled=True)]
    ppermute x0 -> x3, starting transfers between devices: none -> 3.88 us  [the longest x1 3.28 us: ring_gather(): lax.ppermute(going_down, axis, [(d, (d - 1) % ways) for d in range(ways)])]
    all_to_all x1 -> x0, starting transfers between devices: 3.28 us -> none  [per_device(): lax.all_to_all(rounded, 'sec', split_axis=0, concat_axis=2, tiled=True)]
    ppermute x0 -> x3, waiting for transfers between devices: none -> 2.43 us  [the longest x2 2.42 us: ring_gather(): lax.ppermute(going_up, axis, [(d, (d + 1) % ways) for d in range(ways)])]
    all_to_all x1 -> x0, waiting for transfers between devices: 1.59 us -> none  [per_device(): lax.all_to_all(rounded, 'sec', split_axis=0, concat_axis=2, tiled=True)]
  transfers between devices with their start and end apart: 5 -> 7, of which waited for: 1 -> 1; matrix products, arithmetic and copies ran while one was open for 18% -> 25% of each run, Pallas kernels for 0% -> 0%
where the time goes in v1:
time: 137 us; the launch traced here: 136 us
  blocking collectives  61.6 us (45%)
  local copies, waits for them, and re-layouts  22.5 us (16%)
  between operations  15.7 us (11%)
  starting transfers between devices  11.5 us (8%)
  matrix products  8.99 us (7%)
  other arithmetic  7.87 us (6%)
  loops' own time  5.55 us (4%)
  waiting for transfers between devices  2.49 us (2%)
    psum x1, blocking collectives, per_device(): lax.psum((self_squares, cross_squares), ('sec', 'tp'))  32.7 us
    all_gather x1, blocking collectives, per_device(): lax.all_gather(self_key, 'ctx', axis=0, tiled=True)  7.02 us
    all_to_all x1, blocking collectives, per_device(): lax.all_to_all(rounded, 'sec', split_axis=0, concat_axis=2, tiled=True)  6.49 us
    all_gather x1, blocking collectives, per_device(): lax.all_gather(self_value, 'ctx', axis=0, tiled=True)  6.16 us
    dynamic_update_slice x2, local copies, waits for them, and re-layouts, ring_gather(): lax.dynamic_update_slice_in_dim(full, going_up, (here - far) % ways * tur...  5.29 us
    all_gather x1, blocking collectives, per_device(): lax.all_gather(memory_values, 'ctx', axis=0, tiled=True)  4.58 us
    all_gather x1, blocking collectives, per_device(): lax.all_gather(memory_keys, 'ctx', axis=0, tiled=True)  4.58 us
    all_to_all x1, starting transfers between devices, per_device(): lax.all_to_all(own_heads(memory_key), 'sec', split_axis=1, concat_axis=0,...  4.26 us
  transfers between devices with their start and end apart: 7, of which 1 were waited for; matrix products, arithmetic and copies ran while one was open for 25% of the time, Pallas kernels for 0%

profile of v1, /device:TPU:0, one launch (start us, length us, event | category | flops | bytes accessed | tf_op | source)
XLA Modules:
  0.0 136.2 jit_solution(13335472457339134669)
XLA Ops:
  7.2 1.0 reshape.417
  8.9 4.3 %all-to-all-start.1 = ((bf16[32,4,128]{2,0,1:T(8,128)(2,1)}), bf16[32,4,128]{2,0,1:T(8,128)(2,1)S(1)}, u32[]{:S(2)}, u32[]{:S(2)}) async-start(bf16[32,4,128]{2,0,1:T(8,128)(2,1)} %bitcast.165), calls=%async_computation.1 | async-start | bytes 65536 | tf_op jit(solution)/shard_map/all_to_all | solution.py:255
  13.2 1.0 reshape.414
  15.6 7.0 %all_gather.13 = bf16[1024,128]{1,0:T(8,128)(2,1)S(1)} all-gather(bf16[512,128]{1,0:T(8,128)(2,1)} %param.22), channel_id=1, replica_groups=mesh['sec'=4,'ctx'=2,'tp'=4] {'ctx'}, dimensions={0}, use_global_device_ids=true | all-gather | bytes 393216 | tf_op jit(solution)/shard_map/all_gather | solution.py:237
  25.3 6.2 %all_gather.12 = bf16[1024,128]{1,0:T(8,128)(2,1)S(1)} all-gather(bf16[512,128]{1,0:T(8,128)(2,1)} %param.23), channel_id=1, replica_groups=mesh['sec'=4,'ctx'=2,'tp'=4] {'ctx'}, dimensions={0}, use_global_device_ids=true | all-gather | bytes 393216 | tf_op jit(solution)/shard_map/all_gather | solution.py:238
  31.4 2.2 %conditional.3 = (f32[1,512]{1,0:T(1,128)S(1)}, f32[1,512]{1,0:T(1,128)S(1)}) conditional(s32[]{:T(128)} %convert_element_type.106, (s32[1024]{0:T(1024)S(1)}, s32[512]{0:T(512)S(1)}, bf16[512,1,128]{2,0,1:T(8,128)(2,1)}, bf16[1024,128]{1,0:T(8,128)(2,1)S(1)}, f32[1,512]{1,0:T(1,128)S(1)}, /*index=5*/f32[1,512]{1,0:T(1,128)S(1)}) %tuple.182, ...), branch_computations={%region_4.7_spmd, %region_7.8_spmd} | conditional | flops 138937344 | bytes 4622352 | solution.py:78
  31.4 1.5 %fusion = (f32[512]{0:T(512)S(1)}, f32[512,1024]{1,0:T(8,128)S(1)}) fusion(s32[1024]{0:T(1024)S(1)} %get-tuple-element.800, s32[512]{0:T(512)S(1)} %get-tuple-element.801, bf16[1024,128]{1,0:T(8,128)(2,1)S(1)} %get-tuple-element.803, bf16[512,1,128]{2,0,1:T(8,128)(2,1)} %get-tuple-element.802), kind=kOutput, calls=%fused_computation.2 | convolution fusion | flops 136314368 | bytes 2498560 | tf_op jit(solution)/shard_map/while/body/eval_jaxpr/cond/branch_0_fun/qhd,khd->hqk/dot_general | solution.py:46
  33.7 7.2 %while.24 = (s32[]{:T(128)}, f32[512,1,128]{0,2,1:T(8,128)S(1)}, s32[8]{0:T(128)S(1)}, s32[]{:T(128)}, bf16[1024,128]{1,0:T(8,128)(2,1)S(1)}, /*index=5*/s32[512...) while((s32[]{:T(128)}, f32[512,1,128]{0,2,1:T(8,128)S(1)}, ...), condition=%wide.region_13.14_spmd, body=%wide.region_8.13_spmd.sunk | while | flops 135621632 | bytes 935197 | solution.py:111
  35.7 1.5 %conditional.6 = (f32[512,1,128]{0,2,1:T(8,128)S(1)}) conditional(s32[]{:T(128)} %convert_element_type.172, (s32[]{:T(128)}, bf16[1024,128]{1,0:T(8,128)(2,1)S(1)}, s32[512]{0:T(512)S(1)}, s32[512]{0:T(512)S(1)}, bf16[1024,128]{1,0:T(8,128)(2,1)S(1)}, /*index=5*/bf16[512,1,128]{2,0,1:T(8,128)(2,1)}, f32[1,512]{1,0:T(1,128)S(1)}, ...), branch_computations={%region_11.11_spmd, %region_12.12_spmd} | conditional | flops 135593984 | bytes 924714 | solution.py:107
  35.8 1.5 %fusion.10 = f32[512,1,128]{0,2,1:T(8,128)S(1)} fusion(f32[512,1,128]{0,2,1:T(8,128)S(1)} %get-tuple-element.807, f32[512]{0:T(512)S(1)} %bitcast.180, s32[512]{0:T(512)S(1)} %get-tuple-element.811, s32[512]{0:T(512)S(1)} %get-tuple-element.810, bf16[512,1,128]{2,0,1:T(8,128)(2,1)} %get-tuple-element.813, bf16[1024,128]{1,0:T(8,128)(2,1)S(1)} %get-tuple-element.812, ...), kind=kOutput, calls=%fused_computation.14 | convolution fusion | flops 135593984 | bytes 924672 | tf_op jit(solution)/shard_map/while/body/eval_jaxpr/cond/branch_0_fun/hqk,khd->qhd/dot_general | solution.py:101
  39.3 1.5 %conditional.6 = (f32[512,1,128]{0,2,1:T(8,128)S(1)}) conditional(s32[]{:T(128)} %convert_element_type.172, (s32[]{:T(128)}, bf16[1024,128]{1,0:T(8,128)(2,1)S(1)}, s32[512]{0:T(512)S(1)}, s32[512]{0:T(512)S(1)}, bf16[1024,128]{1,0:T(8,128)(2,1)S(1)}, /*index=5*/bf16[512,1,128]{2,0,1:T(8,128)(2,1)}, f32[1,512]{1,0:T(1,128)S(1)}, ...), branch_computations={%region_11.11_spmd, %region_12.12_spmd} | conditional | flops 135593984 | bytes 924714 | solution.py:107
  39.3 1.5 %fusion.10 = f32[512,1,128]{0,2,1:T(8,128)S(1)} fusion(f32[512,1,128]{0,2,1:T(8,128)S(1)} %get-tuple-element.807, f32[512]{0:T(512)S(1)} %bitcast.180, s32[512]{0:T(512)S(1)} %get-tuple-element.811, s32[512]{0:T(512)S(1)} %get-tuple-element.810, bf16[512,1,128]{2,0,1:T(8,128)(2,1)} %get-tuple-element.813, bf16[1024,128]{1,0:T(8,128)(2,1)S(1)} %get-tuple-element.812, ...), kind=kOutput, calls=%fused_computation.14 | convolution fusion | flops 135593984 | bytes 924672 | tf_op jit(solution)/shard_map/while/body/eval_jaxpr/cond/branch_0_fun/hqk,khd->qhd/dot_general | solution.py:101
  42.1 3.3 %all-to-all-start = ((bf16[32,4,128]{2,0,1:T(8,128)(2,1)}), bf16[32,4,128]{2,0,1:T(8,128)(2,1)S(1)}, u32[]{:S(2)}, u32[]{:S(2)}) async-start(bf16[32,4,128]{2,0,1:T(8,128)(2,1)} %bitcast.166), calls=%async_computation | async-start | bytes 65536 | tf_op jit(solution)/shard_map/all_to_all | solution.py:256
  45.4 4.6 %all_gather.15 = bf16[256,128]{1,0:T(8,128)(2,1)S(1)} all-gather(bf16[128,128]{1,0:T(8,128)(2,1)S(1)} %bitcast.174), channel_id=1, replica_groups=mesh['sec'=4,'ctx'=2,'tp'=4] {'ctx'}, dimensions={0}, use_global_device_ids=true | all-gather | bytes 98304 | tf_op jit(solution)/shard_map/all_gather | solution.py:266
  50.4 4.6 %all_gather.14 = bf16[256,128]{1,0:T(8,128)(2,1)S(1)} all-gather(bf16[128,128]{1,0:T(8,128)(2,1)S(1)} %bitcast.175), channel_id=1, replica_groups=mesh['sec'=4,'ctx'=2,'tp'=4] {'ctx'}, dimensions={0}, use_global_device_ids=true | all-gather | bytes 98304 | tf_op jit(solution)/shard_map/all_gather | solution.py:267
  55.2 32.7 %all-reduce = (f32[512]{0:T(512)S(1)}, f32[512]{0:T(512)S(1)}, f32[512]{0:T(512)S(1)}, f32[512]{0:T(512)S(1)}) all-reduce(f32[512]{0:T(512)S(1)} %get-tuple-element.924, f32[512]{0:T(512)S(1)} %get-tuple-element.922, f32[512]{0:T(512)S(1)} %get-tuple-element.923, ...), channel_id=1, replica_groups=mesh['sec'=4,'ctx'=2,'tp'=4] {'sec','tp'}, use_global_device_ids=true, to_apply=%region_15.16 | all-reduce | flops 2048 | bytes 16384 | tf_op jit(solution)/shard_map/psum | solution.py:281
  88.9 0.8 copy.85
  89.7 0.9 fusion.68
  90.7 7.5 %while.25 = (s32[]{:T(128)}, f32[512,1,128]{0,2,1:T(8,128)S(1)}, bf16[1024,256]{0,1:T(8,128)(2,1)S(1)}, s32[8]{0:T(128)S(1)}, s32[]{:T(128)}, /*index=5*/bf16[10...) while((s32[]{:T(128)}, f32[512,1,128]{0,2,1:T(8,128)S(1)}, ...), condition=%wide.region_28.29_spmd, body=%wide.region_23.28_spmd.sunk | while | flops 338455552 | bytes 6965629 | solution.py:185
  92.7 1.7 %conditional.7 = ((f32[512,1,128]{0,2,1:T(8,128)S(1)}, bf16[1024,256]{0,1:T(8,128)(2,1)S(1)})) conditional(s32[]{:T(128)} %convert_element_type.173, (s32[]{:T(128)}, bf16[1024,128]{1,0:T(8,128)(2,1)S(1)}, s32[512]{0:T(512)S(1)}, s32[512]{0:T(512)S(1)}, bf16[512,1,128]{2,0,1:T(8,128)(2,1)S(1)}, /*index=5*/f32[1,512]{1,0:T(1,128)S(1)}, ...), branch_computations={%region_26.26_spmd, %region_27.27_spmd} | conditional | flops 338427904 | bytes 6955082 | solution.py:177
  96.5 1.7 %conditional.7 = ((f32[512,1,128]{0,2,1:T(8,128)S(1)}, bf16[1024,256]{0,1:T(8,128)(2,1)S(1)})) conditional(s32[]{:T(128)} %convert_element_type.173, (s32[]{:T(128)}, bf16[1024,128]{1,0:T(8,128)(2,1)S(1)}, s32[512]{0:T(512)S(1)}, s32[512]{0:T(512)S(1)}, bf16[512,1,128]{2,0,1:T(8,128)(2,1)S(1)}, /*index=5*/f32[1,512]{1,0:T(1,128)S(1)}, ...), branch_computations={%region_26.26_spmd, %region_27.27_spmd} | conditional | flops 338427904 | bytes 6955082 | solution.py:177
  98.2 1.0 copy.73
  99.2 0.9 copy.86
  100.3 6.5 %all_to_all.48 = bf16[128,2,1,1,128]{4,1,3,2,0:T(2,128)(2,1)S(1)} all-to-all(bf16[128,2,1,1,128]{4,1,3,2,0:T(2,128)(2,1)S(1)} %copy.76), channel_id=1, replica_groups=mesh['sec'=4,'ctx'=2,'tp'=4] {'sec'}, dimensions={0} | all-to-all | bytes 131072 | tf_op jit(solution)/shard_map/all_to_all | solution.py:333
  107.4 3.3 %collective-permute-start.1 = (bf16[32,2,4,1,128]{4,0,3,2,1:T(8,128)(2,1)S(1)}, bf16[32,2,4,1,128]{4,0,3,2,1:T(8,128)(2,1)S(1)}, u32[]{:S(2)}, u32[]{:S(2)}) collective-permute-start(bf16[32,2,4,1,128]{4,0,3,2,1:T(8,128)(2,1)S(1)} %bitcast.170), channel_id=1, source_target_pairs={{0,3},{1,0},{2,1},{3,2},{4,7},{5,4},{6,5},{7,6},{8,11},{9,8},{10,9... | collective-permute-start | bytes 196616 | tf_op jit(solution)/shard_map/ppermute | solution.py:22
  110.7 2.4 %collective-permute-done = bf16[32,2,4,1,128]{4,0,3,2,1:T(8,128)(2,1)S(1)} collective-permute-done((bf16[32,2,4,1,128]{4,0,3,2,1:T(8,128)(2,1)S(1)}, bf16[32,2,4,1,128]{4,0,3,2,1:T(8,128)(2,1)S(1)}, u32[]{:S(2)}, u32[]{:S(2)}) %collective-permute-start) | collective-permute-done | bytes 65568 | tf_op jit(solution)/shard_map/ppermute | solution.py:19
  113.4 0.8 copy.83
  115.8 2.6 %dynamic_update_slice.20 = bf16[32,2,4,4,128]{4,3,2,0,1:T(4,128)(2,1)S(1)} dynamic-update-slice(bf16[32,2,4,4,128]{4,3,2,0,1:T(4,128)(2,1)S(1)} %broadcast_in_dim.169, bf16[32,2,4,1,128]{4,3,2,0,1:T(2,128)(2,1)S(1)} %copy.78, s32[]{:T(128)} %constant.403.clone.1, s32[]{:T(128)} %constant.403.clone.1, s32[]{:T(128)} %constant.403.clone.1, s32[]{:T(128)S(6)} %select_n.222, s32[]{:T(128)} %constant.403.clone.1) | dynamic-update-slice | bytes 131076 | tf_op jit(solution)/shard_map/dynamic_update_slice | solution.py:16
  118.6 2.6 %dynamic_update_slice.21 = bf16[32,2,4,4,128]{4,3,2,0,1:T(4,128)(2,1)S(1)} dynamic-update-slice(bf16[32,2,4,4,128]{4,3,2,0,1:T(4,128)(2,1)S(1)} %dynamic_update_slice.20, bf16[32,2,4,1,128]{4,3,2,0,1:T(2,128)(2,1)S(1)} %copy.79, s32[]{:T(128)} %constant.403.clone.1, s32[]{:T(128)} %constant.403.clone.1, s32[]{:T(128)} %constant.403.clone.1, s32[]{:T(128)S(6)} %select_n.224, s32[]{:T(128)} %constant.403.clone.1) | dynamic-update-slice | bytes 131076 | tf_op jit(solution)/shard_map/dynamic_update_slice | solution.py:20
  121.4 2.6 %dynamic_update_slice.22 = bf16[32,2,4,4,128]{4,3,2,0,1:T(4,128)(2,1)S(1)} dynamic-update-slice(bf16[32,2,4,4,128]{4,3,2,0,1:T(4,128)(2,1)S(1)} %dynamic_update_slice.21, bf16[32,2,4,1,128]{4,3,2,0,1:T(2,128)(2,1)S(1)} %copy.80, s32[]{:T(128)} %constant.403.clone.1, s32[]{:T(128)} %constant.403.clone.1, s32[]{:T(128)} %constant.403.clone.1, s32[]{:T(128)S(6)} %select_n.226, s32[]{:T(128)} %constant.403.clone.1) | dynamic-update-slice | bytes 131076 | tf_op jit(solution)/shard_map/dynamic_update_slice | solution.py:23
  124.1 2.6 %dynamic_update_slice.23 = bf16[32,2,4,4,128]{4,3,2,0,1:T(4,128)(2,1)S(1)} dynamic-update-slice(bf16[32,2,4,4,128]{4,3,2,0,1:T(4,128)(2,1)S(1)} %dynamic_update_slice.22, bf16[32,2,4,1,128]{4,3,2,0,1:T(2,128)(2,1)S(1)} %copy.81, s32[]{:T(128)} %constant.403.clone.1, s32[]{:T(128)} %constant.403.clone.1, s32[]{:T(128)} %constant.403.clone.1, s32[]{:T(128)S(6)} %select_n.228, s32[]{:T(128)} %constant.403.clone.1) | dynamic-update-slice | bytes 131076 | tf_op jit(solution)/shard_map/dynamic_update_slice | solution.py:20
  127.7 1.7 %fusion.90 = (bf16[512,128]{1,0:T(8,128)(2,1)}, bf16[512,128]{1,0:T(8,128)(2,1)}) fusion(bf16[512,256]{1,0:T(8,128)(2,1)} %reduce-scatter.5.cloned.1.call-done), kind=kLoop, calls=%fused_computation.160 | loop fusion | bytes 524288 | tf_op jit(solution)/shard_map/slice | solution.py:316
  (95 shorter events, 17.1 us)
Async XLA Ops:
  7.2 42.8 %copy-start = (bf16[512,128]{1,0:T(8,128)(2,1)S(1)}, bf16[512,128]{1,0:T(8,128)(2,1)}, u32[]{:S(2)}) copy-start(bf16[512,128]{1,0:T(8,128)(2,1)} %param.26) | copy-start | bytes 393220
  8.9 33.2 %all-to-all-start.1 = ((bf16[32,4,128]{2,0,1:T(8,128)(2,1)}), bf16[32,4,128]{2,0,1:T(8,128)(2,1)S(1)}, u32[]{:S(2)}, u32[]{:S(2)}) async-start(bf16[32,4,128]{2,0,1:T(8,128)(2,1)} %bitcast.165), calls=%async_computation.1 | async-start | bytes 65536 | tf_op jit(solution)/shard_map/all_to_all | solution.py:255
  31.4 2.2 %copy-start.4 = (s32[8]{0:T(128)S(1)}, s32[8]{0:T(128)}, u32[]{:S(2)}) copy-start(s32[8]{0:T(128)} %param.31) | copy-start | bytes 100
  33.6 7.4 %copy-start.2 = (bf16[512,128]{1,0:T(8,128)(2,1)S(1)}, bf16[512,128]{1,0:T(8,128)(2,1)}, u32[]{:S(2)}) copy-start(bf16[512,128]{1,0:T(8,128)(2,1)} %param.25) | copy-start | bytes 393220
  33.6 7.4 %copy-start.6 = (f32[128]{0:T(128)S(1)}, f32[128]{0:T(128)}, u32[]{:S(2)}) copy-start(f32[128]{0:T(128)} %param.24) | copy-start | bytes 1540
  33.7 8.3 %copy-start.3 = (bf16[512,128]{1,0:T(8,128)(2,1)S(1)}, bf16[512,128]{1,0:T(8,128)(2,1)}, u32[]{:S(2)}) copy-start(bf16[512,128]{1,0:T(8,128)(2,1)} %param.30) | copy-start | bytes 393220
  40.9 14.1 %copy-start.5 = (f32[128]{0:T(128)S(1)}, f32[128]{0:T(128)}, u32[]{:S(2)}) copy-start(f32[128]{0:T(128)} %param.29) | copy-start | bytes 1540
  42.1 8.3 %all-to-all-start = ((bf16[32,4,128]{2,0,1:T(8,128)(2,1)}), bf16[32,4,128]{2,0,1:T(8,128)(2,1)S(1)}, u32[]{:S(2)}, u32[]{:S(2)}) async-start(bf16[32,4,128]{2,0,1:T(8,128)(2,1)} %bitcast.166), calls=%async_computation | async-start | bytes 65536 | tf_op jit(solution)/shard_map/all_to_all | solution.py:256
  45.4 53.9 %reduce-scatter.7.cloned.1.call-start = ((), (), s32[]{:S(2)}) async-start(), calls=%async_computation.6 | async-start | bytes 196608
  88.1 2.5 %copy-start.1 = (bf16[512,1,128]{2,0,1:T(8,128)(2,1)S(1)}, bf16[512,1,128]{2,0,1:T(8,128)(2,1)}, u32[]{:S(2)}) copy-start(bf16[512,1,128]{2,0,1:T(8,128)(2,1)} %get-tuple-element.1228) | copy-start | bytes 393220
  89.7 38.0 %reduce-scatter.5.cloned.1.call-start = ((), (), s32[]{:S(2)}) async-start(), calls=%async_computation.5 | async-start | bytes 786432 | tf_op jit(solution)/shard_map/reduce_scatter | solution.py:312
  106.8 6.3 %collective-permute-start = (bf16[32,2,4,1,128]{4,0,3,2,1:T(8,128)(2,1)S(1)}, bf16[32,2,4,1,128]{4,0,3,2,1:T(8,128)(2,1)S(1)}, u32[]{:S(2)}, u32[]{:S(2)}) collective-permute-start(bf16[32,2,4,1,128]{4,0,3,2,1:T(8,128)(2,1)S(1)} %bitcast.169), channel_id=1, source_target_pairs={{0,1},{1,2},{2,3},{3,0},{4,5},{5,6},{6,7},{7,4},{8,9},{9,10},{10,1... | collective-permute-start | bytes 196616 | tf_op jit(solution)/shard_map/ppermute | solution.py:19
  107.4 13.8 %collective-permute-start.1 = (bf16[32,2,4,1,128]{4,0,3,2,1:T(8,128)(2,1)S(1)}, bf16[32,2,4,1,128]{4,0,3,2,1:T(8,128)(2,1)S(1)}, u32[]{:S(2)}, u32[]{:S(2)}) collective-permute-start(bf16[32,2,4,1,128]{4,0,3,2,1:T(8,128)(2,1)S(1)} %bitcast.170), channel_id=1, source_target_pairs={{0,3},{1,0},{2,1},{3,2},{4,7},{5,4},{6,5},{7,6},{8,11},{9,8},{10,9... | collective-permute-start | bytes 196616 | tf_op jit(solution)/shard_map/ppermute | solution.py:22
  113.1 10.9 %collective-permute-start.2 = (bf16[32,2,4,1,128]{4,0,3,2,1:T(8,128)(2,1)S(1)}, bf16[32,2,4,1,128]{4,0,3,2,1:T(8,128)(2,1)S(1)}, u32[]{:S(2)}, u32[]{:S(2)}) collective-permute-start(bf16[32,2,4,1,128]{4,0,3,2,1:T(8,128)(2,1)S(1)} %collective-permute-done), channel_id=1, source_target_pairs={{0,1},{1,2},{2,3},{3,0},{4,5},{5,6},{6,7},{7,4},{8,9},{9,10},{10,1... | collective-permute-start | bytes 196616 | tf_op jit(solution)/shard_map/ppermute | solution.py:19
Sparse Core Ops, SparseCore 0:
  89.8 8.1 reduce-scatter.6
  100.3 14.6 reduce-scatter.4
